TPU v7x, 256 devices: a whole 4x4x8 slice. The times are simulated.
256 devices in a mesh: req: 32 (over z, x_hi, core), kvh: 4 (over y), exp: 2 (over x_lo).
Axes of the slice: x: 4 (x_hi: 2, x_lo: 2; x = x_hi * 2 + x_lo), y: 4, z: 8, core: 2. Of those that a mesh axis runs over, the one named last changes fastest.
Arguments:
- queries: bfloat16 [4096, 2048], P(('req', 'exp'), 'kvh'), may hold values from -170 to 170
- keys: bfloat16 [4096, 4, 64, 128], P(('req', 'exp'), 'kvh'), may hold values from -6 to 6
- values: bfloat16 [4096, 4, 64, 128], P(('req', 'exp'), 'kvh'), may hold values from -6 to 6
- lengths: int32 [4096], P('req'), may hold values from 2 to 64
- out_weight: bfloat16 [2048, 2048], P(('kvh', 'exp')), may hold values from -0.125 to 0.125
- residual: bfloat16 [4096, 2048], P('req'), may hold values from -54 to 54
- norm_gain: float32 [2048], replicated, may hold values from 0.5 to 2
- expert_ids: int32 [4096, 8], P('req'), may hold values from 0 to 63, as said below
- gate_weights: float32 [4096, 8], P('req'), may hold values from 0.2 to 1
- replica_map: int32 [128], replicated, may hold values from 0 to 63, as said below
- w_gate: bfloat16 [128, 2048, 384], P(('req', 'kvh'), None, 'exp')
- w_up: bfloat16 [128, 2048, 384], P(('req', 'kvh'), None, 'exp')
- w_down: bfloat16 [128, 384, 2048], P(('req', 'kvh'), 'exp')
Outputs:
- layer_out: bfloat16 [4096, 2048], P('req', ('kvh', 'exp'))
Inputs may be any that keep to these rules, and one draw needn't show every extreme that they name: `replica_map`: every one of the 64 experts is served by one or more slots; slots that serve one expert hold equal weights in w_gate, w_up and w_down. `expert_ids`: A token names 8 different experts and every expert is named by some token; among the 128 tokens of one req index no expert is named by more than 24 tokens, and in every req index some expert is named by exactly 24.
All inputs are finite; a program needn't handle non-finite values.
Results may differ from a plain program's by a relative error of at most 0.008.
Values may be sent and summed in bfloat16 or wider, within the bound.
A program may use at most 64 MiB of HBM per device.

v0:
```python
import jax
import jax.numpy as jnp
from jax import lax
from jax.sharding import PartitionSpec as P


def expert_runner(w_gate, w_up, w_down, complete, n_kvh, n_exp, block):

    def run(received):
        full = complete(received)
        lead_a = full.shape[0]
        lead_b = full.shape[1]
        d_model = w_gate.shape[1]
        rows = full.reshape(lead_a * lead_b, d_model)
        gate = jnp.dot(rows, w_gate[0], preferred_element_type=jnp.float32)
        up = jnp.dot(rows, w_up[0], preferred_element_type=jnp.float32)
        act = (jax.nn.silu(gate) * up).astype(jnp.bfloat16)
        down = jnp.dot(act, w_down[0], preferred_element_type=jnp.float32)
        terms = down.reshape(lead_a, lead_b, n_kvh, n_exp, block)
        summed = lax.psum_scatter(
            terms.astype(jnp.bfloat16), "exp", scatter_dimension=3, tiled=True
        )
        back = summed.reshape(lead_a, lead_b, n_kvh * block)
        return lax.all_to_all(back, "req", split_axis=0, concat_axis=0, tiled=True)

    return run


def shards(
    queries,
    keys,
    values,
    lengths,
    out_weight,
    residual,
    norm_gain,
    expert_ids,
    gate_weights,
    replica_map,
    w_gate,
    w_up,
    w_down,
):
    f32 = jnp.float32
    half_rows_count = queries.shape[0]
    n_rows = lengths.shape[0]
    head_dim = keys.shape[3]
    span = keys.shape[2]
    heads_here = queries.shape[1] // head_dim
    n_kvh = lax.axis_size("kvh")
    n_exp = lax.axis_size("exp")
    n_req = lax.axis_size("req")
    side = lax.axis_index("exp")
    own_lengths = lax.dynamic_slice_in_dim(lengths, side * half_rows_count, half_rows_count, 0)
    query = queries.reshape(half_rows_count, heads_here, head_dim)
    scores = jnp.einsum(
        "rhd,rpd->rhp", query, keys[:, 0], preferred_element_type=f32
    ) * head_dim ** (-0.5)
    position = lax.broadcasted_iota(jnp.int32, (1, 1, span), 2)
    valid = position < own_lengths[:, None, None]
    scores = jnp.where(valid, scores, -1e30)
    peak = jnp.max(scores, axis=-1)
    weights = jnp.where(valid, jnp.exp(scores - peak[..., None]), 0.0)
    total = jnp.sum(weights, axis=-1)
    probs = weights / total[..., None]
    numer = jnp.einsum(
        "rhp,rpd->rhd", probs, values[:, 0].astype(f32), precision=lax.Precision.HIGHEST
    )
    attended_part = numer.astype(jnp.bfloat16).reshape(half_rows_count, heads_here * head_dim)
    attended = lax.all_gather(attended_part, "exp", axis=0, tiled=True)
    cut = out_weight.shape[0]
    own_heads = lax.dynamic_slice_in_dim(attended, side * cut, cut, 1)
    d_model = out_weight.shape[1]
    block = d_model // (n_kvh * n_exp)
    attn_block = (
        lax.psum_scatter(
            lax.dot_general(
                out_weight, own_heads, (((0,), (1,)), ((), ())), preferred_element_type=f32
            ).astype(jnp.bfloat16),
            ("kvh", "exp"),
            scatter_dimension=0,
            tiled=True,
        )
        .astype(jnp.float32)
        .T
    )
    offset = lax.axis_index(("kvh", "exp")) * block
    mixed = lax.dynamic_slice_in_dim(residual, offset, block, 1).astype(f32) + attn_block
    squares = lax.psum(jnp.sum(mixed * mixed, axis=1), ("kvh", "exp"))
    scale = lax.rsqrt(squares / d_model + 1e-06)
    gain_block = lax.dynamic_slice_in_dim(norm_gain, offset, block, 0)
    normed = (mixed * scale[:, None] * gain_block[None, :]).astype(jnp.bfloat16)
    top = expert_ids.shape[1]
    n_slots = replica_map.shape[0]
    n_experts = n_slots // 2
    capacity = min(n_rows, max(2, (3 * n_rows * top + 2 * n_experts - 1) // (2 * n_experts)))
    probs_top = gate_weights / jnp.sum(gate_weights, axis=1, keepdims=True)
    expert_range = jnp.arange(n_experts, dtype=jnp.int32)
    owned = (replica_map[:, None] == expert_range[None, :]).astype(jnp.int32)
    earlier = jnp.cumsum(owned, axis=0) - owned
    rank = jnp.sum(earlier * owned, axis=1)
    copies = jnp.sum(owned, axis=0)
    picked = (expert_ids[..., None] == expert_range).astype(jnp.int32)
    copies_pair = jnp.sum(picked * copies, axis=-1)
    turn = jnp.full((n_rows, top), lax.axis_index("req"), jnp.int32)
    which = turn % copies_pair
    match = (replica_map == expert_ids[..., None]) & (rank == which[..., None])
    slot = jnp.argmax(match, axis=-1)
    mine = slot % n_kvh == lax.axis_index("kvh")
    flat_dest = (slot // n_kvh).reshape(-1)
    flat_mine = mine.reshape(-1)
    toward = (
        (flat_dest[:, None] == jnp.arange(n_req, dtype=jnp.int32)[None, :]) & flat_mine[:, None]
    ).astype(jnp.int32)
    before = jnp.cumsum(toward, axis=0) - toward
    place = jnp.sum(before * toward, axis=1)
    n_buffer = n_req * capacity
    target = jnp.where(flat_mine, flat_dest * capacity + place, n_buffer)
    row_of = jnp.arange(n_rows * top, dtype=jnp.int32) // top
    source = jnp.full((n_buffer,), -1, jnp.int32).at[target].set(row_of, mode="drop")
    full_rows = lax.all_gather(normed, ("kvh", "exp"), axis=1, tiled=True)

    def keep(received):
        return received

    runner = expert_runner(w_gate, w_up, w_down, keep, n_kvh, n_exp, block)
    taken = full_rows[jnp.maximum(source, 0)]
    returned = runner(
        lax.all_to_all(
            jnp.where(source[:, None] >= 0, taken, jnp.zeros((), jnp.bfloat16)).reshape(
                n_req, capacity, full_rows.shape[1]
            ),
            "req",
            split_axis=0,
            concat_axis=0,
            tiled=True,
        )
    )
    flat_back = returned.reshape(n_buffer, n_kvh * block)
    gathered = flat_back[jnp.minimum(target, n_buffer - 1)].reshape(n_rows, top, n_kvh * block)
    weight = jnp.where(mine, probs_top, 0.0)
    partial_value = jnp.zeros((n_rows, n_kvh * block), f32)
    for entry in range(top):
        partial_value = partial_value + weight[:, entry, None] * gathered[:, entry].astype(f32)
    moe_block = (
        lax.psum_scatter(
            partial_value.reshape(n_rows, n_kvh, block).astype(jnp.bfloat16),
            "kvh",
            scatter_dimension=1,
            tiled=True,
        )
        .astype(jnp.float32)
        .reshape(n_rows, block)
    )
    return (mixed + moe_block).astype(jnp.bfloat16)


def solution(mesh):
    in_specs = (
        P(("req", "exp"), "kvh"),
        P(("req", "exp"), "kvh", None, None),
        P(("req", "exp"), "kvh", None, None),
        P("req"),
        P(("kvh", "exp"), None),
        P("req", None),
        P(),
        P("req", None),
        P("req", None),
        P(),
        P(("req", "kvh"), None, "exp"),
        P(("req", "kvh"), None, "exp"),
        P(("req", "kvh"), "exp", None),
    )
    out_specs = P("req", ("kvh", "exp"))
    return jax.shard_map(shards, mesh=mesh, in_specs=in_specs, out_specs=out_specs, check_vma=False)
```

profile of v0, /device:TPU:2, one launch (start us, length us, event | category | flops | bytes accessed | tf_op | source)
XLA Modules:
  0.0 418.7 jit_solution(3520700671279704682)
XLA Ops:
  10.4 2.2 convolution_convert_fusion.2
  12.6 5.2 %all_gather.6 = bf16[128,512]{1,0:T(8,128)(2,1)S(1)} all-gather(bf16[64,512]{1,0:T(8,128)(2,1)S(1)} %bitcast.127), channel_id=1, replica_groups=mesh['req'=32,'kvh'=4,'exp'=2] {'exp'}, dimensions={0}, use_global_device_ids=true | all-gather | bytes 196608 | tf_op jit(solution)/shard_map/all_gather | solution.py:70
  19.9 5.6 %iota_reduce_fusion = (pred[128,8]{1,0:T(8,128)(4,1)}, s32[128,8]{1,0:T(8,128)S(1)}) fusion(s32[128,8]{1,0:T(8,128)S(1)} %copy.92, s32[128]{0:T(128)S(1)} %get-tuple-element.7, s32[128,8]{1,0:T(8,128)S(1)} %copy.91, s32[128]{0:T(128)S(1)} %copy-done.5), kind=kLoop, calls=%fused_computation.24 | loop fusion | flops 1303552 | bytes 14336 | tf_op jit(solution)/shard_map/shards/reduce | solution.py:108
  26.0 9.0 %reduce-window.6 = s32[32,8,128]{2,1,0:T(8,128)S(1)} reduce-window(s32[32,8,128]{2,1,0:T(8,128)S(1)} %fusion.21, s32[]{:T(128)} %constant.89.clone.1), window={size=1x1x128 pad=0_0x0_0x127_0}, to_apply=%region_9.10 | reduce-window | flops 4161536 | bytes 262148 | tf_op jit(solution)/shard_map/reduce-window
  36.1 4.3 %scatter_custom_fusion = s32[768]{0:T(1024)S(1)} fusion(s32[1024]{0:T(1024)S(1)} %bitcast.132, s32[1024]{0:T(1024)S(1)} %add_select_fusion, s32[]{:T(128)} %constant.107.clone.1), kind=kCustom, calls=%fused_computation.82 | custom fusion | bytes 3076 | tf_op jit(solution)/shard_map/scatter | solution.py:120
  41.3 18.5 %reduce-scatter.4.cloned.1.call-done = bf16[256,128]{0,1:T(8,128)(2,1)} async-done(((bf16[2048,128]{0,1:T(8,128)(2,1)}), bf16[256,128]{0,1:T(8,128)(2,1)}) %reduce-scatter.4.cloned.1.call-update) | async-done | bytes 65552 | tf_op jit(solution)/shard_map/reduce_scatter | solution.py:76
  60.8 19.4 %psum.7 = f32[128]{0:T(128)S(1)} all-reduce(f32[128]{0:T(128)S(1)} %multiply_reduce_fusion), channel_id=1, replica_groups=mesh['req'=32,'kvh'=4,'exp'=2] {'kvh','exp'}, use_global_device_ids=true, to_apply=%region_14.15 | all-reduce | flops 128 | bytes 1024 | tf_op jit(solution)/shard_map/psum | solution.py:89
  81.2 28.2 %all_gather.7 = bf16[128,2048]{1,0:T(8,128)(2,1)S(1)} all-gather(bf16[128,256]{1,0:T(8,128)(2,1)S(1)} %multiply_convert_fusion), channel_id=1, replica_groups=mesh['req'=32,'kvh'=4,'exp'=2] {'kvh','exp'}, dimensions={1}, use_global_device_ids=true | all-gather | bytes 589824 | tf_op jit(solution)/shard_map/all_gather | solution.py:121
  109.4 4.3 %gather_fusion = bf16[768,2048]{1,0:T(8,128)(2,1)} fusion(bf16[128,2048]{1,0:T(8,128)(2,1)S(1)} %all_gather.7, s32[1024]{0:T(1024)S(1)} %pad_clamp_fusion), kind=kCustom, calls=%fused_computation | custom fusion | bytes 6294528 | tf_op jit(solution)/shard_map/gather | solution.py:127
  113.7 3.8 broadcast_select_fusion
  117.5 8.9 %all-to-all-start = ((bf16[32,24,2048]{2,1,0:T(8,128)(2,1)}), bf16[32,24,2048]{2,1,0:T(8,128)(2,1)}, u32[]{:S(2)}, u32[]{:S(2)}) async-start(bf16[32,24,2048]{2,1,0:T(8,128)(2,1)} %broadcast_select_fusion), calls=%async_computation.1 | async-start | bytes 6291456 | tf_op jit(solution)/shard_map/all_to_all | solution.py:129
  127.2 73.4 %all-to-all-done = bf16[32,24,2048]{2,1,0:T(8,128)(2,1)} async-done(((bf16[32,24,2048]{2,1,0:T(8,128)(2,1)}), bf16[32,24,2048]{2,1,0:T(8,128)(2,1)}, u32[]{:S(2)}, u32[]{:S(2)}) %all-to-all-start) | async-done | bytes 3145760 | tf_op jit(solution)/shard_map/all_to_all | solution.py:129
  200.6 3.2 fusion.11
  203.8 3.1 fusion.2
  207.1 2.7 convolution_convert_fusion.1
  210.4 92.4 %all-reduce.3.cloned.1.call-done = bf16[32,24,4,2,256]{4,1,3,2,0:T(8,128)(2,1)} async-done(((bf16[32,24,4,2,256]{4,1,3,2,0:T(8,128)(2,1)}), bf16[32,24,4,2,256]{4,1,3,2,0:T(8,128)(2,1)}) %all-reduce.3.cloned.1.call-update) | async-done | bytes 3145744
  302.8 2.2 constant_dynamic-slice_fusion
  305.8 2.4 reshape.238
  308.1 9.5 %all-to-all-start.1 = ((bf16[32,24,1024]{2,1,0:T(8,128)(2,1)}), bf16[32,24,1024]{2,1,0:T(8,128)(2,1)S(1)}, u32[]{:S(2)}, u32[]{:S(2)}) async-start(bf16[32,24,1024]{2,1,0:T(8,128)(2,1)} %reshape.238), calls=%async_computation.2 | async-start | bytes 3145728 | tf_op jit(solution)/shard_map/all_to_all | solution.py:24
  317.7 39.4 %all-to-all-done.1 = bf16[32,24,1024]{2,1,0:T(8,128)(2,1)S(1)} async-done(((bf16[32,24,1024]{2,1,0:T(8,128)(2,1)}), bf16[32,24,1024]{2,1,0:T(8,128)(2,1)S(1)}, u32[]{:S(2)}, u32[]{:S(2)}) %all-to-all-start.1) | async-done | bytes 1572896 | tf_op jit(solution)/shard_map/all_to_all | solution.py:24
  357.0 5.4 %gather_fusion.1 = bf16[1024,1024]{1,0:T(8,128)(2,1)} fusion(bf16[768,1024]{1,0:T(8,128)(2,1)S(1)} %bitcast.113, s32[1024]{0:T(1024)S(1)} %broadcast_clamp_fusion), kind=kCustom, calls=%fused_computation.1 | custom fusion | bytes 4198400 | tf_op jit(solution)/shard_map/gather | solution.py:140
  362.4 12.5 %fusion.38 = (bf16[128,1,1024]{2,1,0:T(2,128)(2,1)S(1)}, bf16[128,1,1024]{2,1,0:T(2,128)(2,1)}, bf16[128,1,1024]{2,1,0:T(2,128)(2,1)}, bf16[128,1,1024]{2,1,0:T(...) fusion(bf16[128,8,1024]{2,1,0:T(8,128)(2,1)} %bitcast.114), kind=kLoop, calls=%fused_computation.95 | loop fusion | bytes 4194304 | tf_op jit(solution)/shard_map/slice | solution.py:144
  386.3 2.6 add_convert_fusion
  388.9 21.7 %reduce-scatter.6.cloned.1.call-done = bf16[128,1,256]{2,0,1:T(8,128)(2,1)} async-done(((bf16[128,4,256]{2,0,1:T(8,128)(2,1)}), bf16[128,1,256]{2,0,1:T(8,128)(2,1)}) %reduce-scatter.6.cloned.1.call-update) | async-done | bytes 65552 | tf_op jit(solution)/shard_map/reduce_scatter | solution.py:146
  (91 shorter events, 25.5 us)
Async XLA Ops:
  6.5 11.3 %copy-start = (bf16[256,2048]{1,0:T(8,128)(2,1)S(1)}, bf16[256,2048]{1,0:T(8,128)(2,1)}, u32[]{:S(2)}) copy-start(bf16[256,2048]{1,0:T(8,128)(2,1)} %param.17) | copy-start | bytes 3145732
  6.5 12.4 %copy-start.5 = (s32[128]{0:T(128)S(1)}, s32[128]{0:T(128)}, u32[]{:S(2)}) copy-start(s32[128]{0:T(128)} %param.22) | copy-start | bytes 1540
  6.5 12.9 %copy-start.4 = (s32[128,8]{0,1:T(8,128)S(1)}, s32[128,8]{0,1:T(8,128)}, u32[]{:S(2)}) copy-start(s32[128,8]{0,1:T(8,128)} %param.20) | copy-start | bytes 12292
  6.5 19.0 %copy-start.3 = (f32[128,8]{0,1:T(8,128)S(1)}, f32[128,8]{0,1:T(8,128)}, u32[]{:S(2)}) copy-start(f32[128,8]{0,1:T(8,128)} %param.21) | copy-start | bytes 12292
  6.5 53.3 %reduce-scatter.4.cloned.1.call-start = ((), (), s32[]{:S(2)}) async-start(), calls=%async_computation.4 | async-start | bytes 589824 | tf_op jit(solution)/shard_map/reduce_scatter | solution.py:76
  117.5 9.1 %copy-start.1 = (bf16[1,192,2048]{2,1,0:T(8,128)(2,1)S(1)}, bf16[1,192,2048]{2,1,0:T(8,128)(2,1)}, u32[]{:S(2)}) copy-start(bf16[1,192,2048]{2,1,0:T(8,128)(2,1)} %param.25) | copy-start | bytes 2359300
  117.5 83.1 %copy-start.6 = (bf16[1,2048,192]{1,2,0:T(8,128)(2,1)S(1)}, bf16[1,2048,192]{1,2,0:T(8,128)(2,1)}, u32[]{:S(2)}) copy-start(bf16[1,2048,192]{1,2,0:T(8,128)(2,1)} %param.23) | copy-start | bytes 2359300
  117.5 83.1 %all-to-all-start = ((bf16[32,24,2048]{2,1,0:T(8,128)(2,1)}), bf16[32,24,2048]{2,1,0:T(8,128)(2,1)}, u32[]{:S(2)}, u32[]{:S(2)}) async-start(bf16[32,24,2048]{2,1,0:T(8,128)(2,1)} %broadcast_select_fusion), calls=%async_computation.1 | async-start | bytes 6291456 | tf_op jit(solution)/shard_map/all_to_all | solution.py:129
  126.4 176.5 %all-reduce.3.cloned.1.call-start = ((), (), s32[]{:S(2)}) async-start(), calls=%async_computation.6 | async-start | bytes 6291456
  200.6 3.2 copy-start.7
  207.1 2.8 copy-start.8
  308.1 48.9 %all-to-all-start.1 = ((bf16[32,24,1024]{2,1,0:T(8,128)(2,1)}), bf16[32,24,1024]{2,1,0:T(8,128)(2,1)S(1)}, u32[]{:S(2)}, u32[]{:S(2)}) async-start(bf16[32,24,1024]{2,1,0:T(8,128)(2,1)} %reshape.238), calls=%async_computation.2 | async-start | bytes 3145728 | tf_op jit(solution)/shard_map/all_to_all | solution.py:24
  317.6 93.0 %reduce-scatter.6.cloned.1.call-start = ((), (), s32[]{:S(2)}) async-start(), calls=%async_computation.5 | async-start | bytes 327680 | tf_op jit(solution)/shard_map/reduce_scatter | solution.py:146
  385.7 24.9 %copy-start.2 = (bf16[256,128]{0,1:T(8,128)(2,1)S(1)}, bf16[256,128]{0,1:T(8,128)(2,1)}, u32[]{:S(2)}) copy-start(bf16[256,128]{0,1:T(8,128)(2,1)} %reduce-scatter.4.cloned.1.call-done) | copy-start | bytes 196612
Sparse Core Ops, SparseCore 0:
  19.1 40.6 reduce-scatter.3
  209.9 92.8 all-reduce.2
  389.0 21.5 reduce-scatter.5
where the time goes:
time: 419 us
  waiting for transfers between devices  246 us (59%)
  blocking collectives  52.8 us (13%)
  local copies, waits for them, and re-layouts  48.4 us (12%)
  other arithmetic  25.5 us (6%)
  starting transfers between devices  18.6 us (4%)
  matrix products  14.4 us (3%)
  between operations  13.5 us (3%)
    unnamed x4, waiting for transfers between devices  92.5 us
    all_to_all x1, waiting for transfers between devices, shards(): lax.all_to_all(jnp.where(source[:, None] >= 0, taken, jnp.zeros((), jnp.b...  73.4 us
    all_to_all x1, waiting for transfers between devices, run(): return lax.all_to_all(back, 'req', split_axis=0, concat_axis=0, tiled=True)  39.4 us
    all_gather x1, blocking collectives, shards(): full_rows = lax.all_gather(normed, ('kvh', 'exp'), axis=1, tiled=True)  28.2 us
    reduce_scatter x1, waiting for transfers between devices, shards(): lax.psum_scatter(partial_value.reshape(n_rows, n_kvh, block).astype(jnp.b...  21.7 us
    psum x1, blocking collectives, shards(): squares = lax.psum(jnp.sum(mixed * mixed, axis=1), ('kvh', 'exp'))  19.4 us
    reduce_scatter x1, waiting for transfers between devices, shards(): lax.psum_scatter(lax.dot_general(out_weight, own_heads, (((0,), (1,)), ((...  18.5 us
    slice x1, local copies, waits for them, and re-layouts, shards(): gathered[:, entry].astype(f32)  12.5 us
  transfers between devices with their start and end apart: 5, of which 5 were waited for; matrix products, arithmetic and copies ran while one was open for 6% of the time, Pallas kernels for 0%

commit v1 on v0

--- a/solution.py
+++ b/solution.py
@@ -1,7 +1,23 @@
+import functools
 import jax
 import jax.numpy as jnp
 from jax import lax
 from jax.sharding import PartitionSpec as P
+
+
+def follow_signs_now(local_x, across):
+    return jnp.concatenate(
+        lax.all_to_all(
+            jnp.stack([local_x] * lax.axis_size(across)),
+            axis_name=across,
+            split_axis=0,
+            concat_axis=0,
+        ),
+        axis=1,
+    )
+
+
+finish_frame = functools.partial(follow_signs_now, across=("kvh", "exp"))
 
 
 def expert_runner(w_gate, w_up, w_down, complete, n_kvh, n_exp, block):
@@ -118,7 +134,7 @@
     target = jnp.where(flat_mine, flat_dest * capacity + place, n_buffer)
     row_of = jnp.arange(n_rows * top, dtype=jnp.int32) // top
     source = jnp.full((n_buffer,), -1, jnp.int32).at[target].set(row_of, mode="drop")
-    full_rows = lax.all_gather(normed, ("kvh", "exp"), axis=1, tiled=True)
+    full_rows = finish_frame(normed)
 
     def keep(received):
         return received

time: 419 us -> 403 us (0.962)
  blocking collectives: 52.8 us -> 24.8 us
  waiting for transfers between devices: 246 us -> 252 us
  starting transfers between devices: 18.6 us -> 23.1 us
    all_gather x1 -> x0, blocking collectives: 28.2 us -> none  [shards(): full_rows = lax.all_gather(normed, ('kvh', 'exp'), axis=1, tiled=True)]
    all_to_all x0 -> x1, waiting for transfers between devices: none -> 7.42 us  [follow_signs_now(): lax.all_to_all(jnp.stack([local_x] * lax.axis_size(across)), axis_name=ac...]
  transfers between devices with their start and end apart: 5 -> 6, of which waited for: 5 -> 6; matrix products, arithmetic and copies ran while one was open for 6% -> 6% of each run, Pallas kernels for 0% -> 0%
where the time goes in v1:
time: 403 us; the launch traced here: 402 us
  waiting for transfers between devices  252 us (63%)
  local copies, waits for them, and re-layouts  49.3 us (12%)
  other arithmetic  25.5 us (6%)
  blocking collectives  24.8 us (6%)
  starting transfers between devices  23.1 us (6%)
  matrix products  14.4 us (4%)
  between operations  13.5 us (3%)
    unnamed x4, waiting for transfers between devices  91.1 us
    all_to_all x1, waiting for transfers between devices, shards(): lax.all_to_all(jnp.where(source[:, None] >= 0, taken, jnp.zeros((), jnp.b...  73.4 us
    all_to_all x1, waiting for transfers between devices, run(): return lax.all_to_all(back, 'req', split_axis=0, concat_axis=0, tiled=True)  39.4 us
    reduce_scatter x1, waiting for transfers between devices, shards(): lax.psum_scatter(partial_value.reshape(n_rows, n_kvh, block).astype(jnp.b...  21.7 us
    psum x1, blocking collectives, shards(): squares = lax.psum(jnp.sum(mixed * mixed, axis=1), ('kvh', 'exp'))  19.6 us
    reduce_scatter x1, waiting for transfers between devices, shards(): lax.psum_scatter(lax.dot_general(out_weight, own_heads, (((0,), (1,)), ((...  18.6 us
    slice x1, local copies, waits for them, and re-layouts, shards(): gathered[:, entry].astype(f32)  12.5 us
    unnamed x30, local copies, waits for them, and re-layouts  9.82 us
  transfers between devices with their start and end apart: 6, of which 6 were waited for; matrix products, arithmetic and copies ran while one was open for 6% of the time, Pallas kernels for 0%

profile of v1, /device:TPU:2, one launch (start us, length us, event | category | flops | bytes accessed | tf_op | source)
XLA Modules:
  0.0 402.3 jit_solution(410025781096947493)
XLA Ops:
  10.4 2.2 convolution_convert_fusion.2
  12.6 5.2 %all_gather.3 = bf16[128,512]{1,0:T(8,128)(2,1)S(1)} all-gather(bf16[64,512]{1,0:T(8,128)(2,1)S(1)} %bitcast.132), channel_id=1, replica_groups=mesh['req'=32,'kvh'=4,'exp'=2] {'exp'}, dimensions={0}, use_global_device_ids=true | all-gather | bytes 196608 | tf_op jit(solution)/shard_map/all_gather | solution.py:86
  19.9 5.6 %iota_reduce_fusion = (pred[128,8]{1,0:T(8,128)(4,1)}, s32[128,8]{1,0:T(8,128)S(1)}) fusion(s32[128,8]{1,0:T(8,128)S(1)} %copy.93, s32[128]{0:T(128)S(1)} %get-tuple-element.7, s32[128,8]{1,0:T(8,128)S(1)} %copy.92, s32[128]{0:T(128)S(1)} %copy-done.5), kind=kLoop, calls=%fused_computation.24 | loop fusion | flops 1303552 | bytes 14336 | tf_op jit(solution)/shard_map/shards/reduce | solution.py:124
  26.3 9.0 %reduce-window.6 = s32[32,8,128]{2,1,0:T(8,128)S(1)} reduce-window(s32[32,8,128]{2,1,0:T(8,128)S(1)} %fusion.21, s32[]{:T(128)} %constant.89.clone.1), window={size=1x1x128 pad=0_0x0_0x127_0}, to_apply=%region_9.10 | reduce-window | flops 4161536 | bytes 262148 | tf_op jit(solution)/shard_map/reduce-window
  36.8 4.3 %scatter_custom_fusion = s32[768]{0:T(1024)S(1)} fusion(s32[1024]{0:T(1024)S(1)} %bitcast.137, s32[1024]{0:T(1024)S(1)} %add_select_fusion, s32[]{:T(128)} %constant.107.clone.1), kind=kCustom, calls=%fused_computation.82 | custom fusion | bytes 3076 | tf_op jit(solution)/shard_map/scatter | solution.py:136
  41.1 18.6 %reduce-scatter.4.cloned.1.call-done = bf16[256,128]{0,1:T(8,128)(2,1)} async-done(((bf16[2048,128]{0,1:T(8,128)(2,1)}), bf16[256,128]{0,1:T(8,128)(2,1)}) %reduce-scatter.4.cloned.1.call-update) | async-done | bytes 65552 | tf_op jit(solution)/shard_map/reduce_scatter | solution.py:92
  60.7 19.6 %psum.7 = f32[128]{0:T(128)S(1)} all-reduce(f32[128]{0:T(128)S(1)} %multiply_reduce_fusion), channel_id=1, replica_groups=mesh['req'=32,'kvh'=4,'exp'=2] {'kvh','exp'}, use_global_device_ids=true, to_apply=%region_14.15 | all-reduce | flops 128 | bytes 1024 | tf_op jit(solution)/shard_map/psum | solution.py:105
  82.1 4.0 %all-to-all-start = ((bf16[8,128,256]{2,1,0:T(8,128)(2,1)}), bf16[8,128,256]{2,1,0:T(8,128)(2,1)S(1)}, u32[]{:S(2)}, u32[]{:S(2)}) async-start(bf16[8,128,256]{2,1,0:T(8,128)(2,1)} %stack.2), calls=%async_computation.1 | async-start | bytes 1048576 | tf_op jit(solution)/shard_map/all_to_all | solution.py:10
  86.3 7.4 %all-to-all-done = bf16[8,128,256]{2,1,0:T(8,128)(2,1)S(1)} async-done(((bf16[8,128,256]{2,1,0:T(8,128)(2,1)}), bf16[8,128,256]{2,1,0:T(8,128)(2,1)S(1)}, u32[]{:S(2)}, u32[]{:S(2)}) %all-to-all-start) | async-done | bytes 524320 | tf_op jit(solution)/shard_map/all_to_all | solution.py:10
  93.8 4.3 %gather_fusion = bf16[768,2048]{1,0:T(8,128)(2,1)} fusion(bf16[128,2048]{1,0:T(8,128)(2,1)S(1)} %bitcast.116, s32[1024]{0:T(1024)S(1)} %pad_clamp_fusion), kind=kCustom, calls=%fused_computation | custom fusion | bytes 6294528 | tf_op jit(solution)/shard_map/gather | solution.py:143
  98.0 3.8 broadcast_select_fusion
  101.9 9.3 %all-to-all-start.1 = ((bf16[32,24,2048]{2,1,0:T(8,128)(2,1)}), bf16[32,24,2048]{2,1,0:T(8,128)(2,1)}, u32[]{:S(2)}, u32[]{:S(2)}) async-start(bf16[32,24,2048]{2,1,0:T(8,128)(2,1)} %broadcast_select_fusion), calls=%async_computation.2 | async-start | bytes 6291456 | tf_op jit(solution)/shard_map/all_to_all | solution.py:145
  112.1 73.4 %all-to-all-done.1 = bf16[32,24,2048]{2,1,0:T(8,128)(2,1)} async-done(((bf16[32,24,2048]{2,1,0:T(8,128)(2,1)}), bf16[32,24,2048]{2,1,0:T(8,128)(2,1)}, u32[]{:S(2)}, u32[]{:S(2)}) %all-to-all-start.1) | async-done | bytes 3145760 | tf_op jit(solution)/shard_map/all_to_all | solution.py:145
  185.5 3.1 fusion.11
  188.7 3.1 fusion.2
  192.0 2.7 convolution_convert_fusion.1
  195.3 91.1 %all-reduce.3.cloned.1.call-done = bf16[32,24,4,2,256]{4,1,3,2,0:T(8,128)(2,1)} async-done(((bf16[32,24,4,2,256]{4,1,3,2,0:T(8,128)(2,1)}), bf16[32,24,4,2,256]{4,1,3,2,0:T(8,128)(2,1)}) %all-reduce.3.cloned.1.call-update) | async-done | bytes 3145744
  289.4 2.4 reshape.248
  291.7 9.5 %all-to-all-start.2 = ((bf16[32,24,1024]{2,1,0:T(8,128)(2,1)}), bf16[32,24,1024]{2,1,0:T(8,128)(2,1)S(1)}, u32[]{:S(2)}, u32[]{:S(2)}) async-start(bf16[32,24,1024]{2,1,0:T(8,128)(2,1)} %reshape.248), calls=%async_computation.3 | async-start | bytes 3145728 | tf_op jit(solution)/shard_map/all_to_all | solution.py:40
  301.2 39.4 %all-to-all-done.2 = bf16[32,24,1024]{2,1,0:T(8,128)(2,1)S(1)} async-done(((bf16[32,24,1024]{2,1,0:T(8,128)(2,1)}), bf16[32,24,1024]{2,1,0:T(8,128)(2,1)S(1)}, u32[]{:S(2)}, u32[]{:S(2)}) %all-to-all-start.2) | async-done | bytes 1572896 | tf_op jit(solution)/shard_map/all_to_all | solution.py:40
  340.6 5.4 %gather_fusion.1 = bf16[1024,1024]{1,0:T(8,128)(2,1)} fusion(bf16[768,1024]{1,0:T(8,128)(2,1)S(1)} %bitcast.117, s32[1024]{0:T(1024)S(1)} %broadcast_clamp_fusion), kind=kCustom, calls=%fused_computation.1 | custom fusion | bytes 4198400 | tf_op jit(solution)/shard_map/gather | solution.py:156
  346.0 12.5 %fusion.38 = (bf16[128,1,1024]{2,1,0:T(2,128)(2,1)S(1)}, bf16[128,1,1024]{2,1,0:T(2,128)(2,1)}, bf16[128,1,1024]{2,1,0:T(2,128)(2,1)}, bf16[128,1,1024]{2,1,0:T(...) fusion(bf16[128,8,1024]{2,1,0:T(8,128)(2,1)} %bitcast.118), kind=kLoop, calls=%fused_computation.95 | loop fusion | bytes 4194304 | tf_op jit(solution)/shard_map/slice | solution.py:160
  369.8 2.6 add_convert_fusion
  372.5 21.7 %reduce-scatter.6.cloned.1.call-done = bf16[128,1,256]{2,0,1:T(8,128)(2,1)} async-done(((bf16[128,4,256]{2,0,1:T(8,128)(2,1)}), bf16[128,1,256]{2,0,1:T(8,128)(2,1)}) %reduce-scatter.6.cloned.1.call-update) | async-done | bytes 65552 | tf_op jit(solution)/shard_map/reduce_scatter | solution.py:162
  (94 shorter events, 28.5 us)
Async XLA Ops:
  6.5 11.3 %copy-start = (bf16[256,2048]{1,0:T(8,128)(2,1)S(1)}, bf16[256,2048]{1,0:T(8,128)(2,1)}, u32[]{:S(2)}) copy-start(bf16[256,2048]{1,0:T(8,128)(2,1)} %param.17) | copy-start | bytes 3145732
  6.5 12.4 %copy-start.5 = (s32[128]{0:T(128)S(1)}, s32[128]{0:T(128)}, u32[]{:S(2)}) copy-start(s32[128]{0:T(128)} %param.22) | copy-start | bytes 1540
  6.5 12.9 %copy-start.4 = (s32[128,8]{0,1:T(8,128)S(1)}, s32[128,8]{0,1:T(8,128)}, u32[]{:S(2)}) copy-start(s32[128,8]{0,1:T(8,128)} %param.20) | copy-start | bytes 12292
  6.5 18.9 %copy-start.3 = (f32[128,8]{0,1:T(8,128)S(1)}, f32[128,8]{0,1:T(8,128)}, u32[]{:S(2)}) copy-start(f32[128,8]{0,1:T(8,128)} %param.21) | copy-start | bytes 12292
  6.5 53.2 %reduce-scatter.4.cloned.1.call-start = ((), (), s32[]{:S(2)}) async-start(), calls=%async_computation.5 | async-start | bytes 589824 | tf_op jit(solution)/shard_map/reduce_scatter | solution.py:92
  82.1 11.6 %all-to-all-start = ((bf16[8,128,256]{2,1,0:T(8,128)(2,1)}), bf16[8,128,256]{2,1,0:T(8,128)(2,1)S(1)}, u32[]{:S(2)}, u32[]{:S(2)}) async-start(bf16[8,128,256]{2,1,0:T(8,128)(2,1)} %stack.2), calls=%async_computation.1 | async-start | bytes 1048576 | tf_op jit(solution)/shard_map/all_to_all | solution.py:10
  101.9 9.6 %copy-start.1 = (bf16[1,192,2048]{2,1,0:T(8,128)(2,1)S(1)}, bf16[1,192,2048]{2,1,0:T(8,128)(2,1)}, u32[]{:S(2)}) copy-start(bf16[1,192,2048]{2,1,0:T(8,128)(2,1)} %param.25) | copy-start | bytes 2359300
  101.9 83.6 %copy-start.6 = (bf16[1,2048,192]{1,2,0:T(8,128)(2,1)S(1)}, bf16[1,2048,192]{1,2,0:T(8,128)(2,1)}, u32[]{:S(2)}) copy-start(bf16[1,2048,192]{1,2,0:T(8,128)(2,1)} %param.23) | copy-start | bytes 2359300
  101.9 83.6 %all-to-all-start.1 = ((bf16[32,24,2048]{2,1,0:T(8,128)(2,1)}), bf16[32,24,2048]{2,1,0:T(8,128)(2,1)}, u32[]{:S(2)}, u32[]{:S(2)}) async-start(bf16[32,24,2048]{2,1,0:T(8,128)(2,1)} %broadcast_select_fusion), calls=%async_computation.2 | async-start | bytes 6291456 | tf_op jit(solution)/shard_map/all_to_all | solution.py:145
  111.2 175.2 %all-reduce.3.cloned.1.call-start = ((), (), s32[]{:S(2)}) async-start(), calls=%async_computation.7 | async-start | bytes 6291456
  185.5 3.2 copy-start.7
  191.9 2.8 copy-start.8
  291.7 48.9 %all-to-all-start.2 = ((bf16[32,24,1024]{2,1,0:T(8,128)(2,1)}), bf16[32,24,1024]{2,1,0:T(8,128)(2,1)S(1)}, u32[]{:S(2)}, u32[]{:S(2)}) async-start(bf16[32,24,1024]{2,1,0:T(8,128)(2,1)} %reshape.248), calls=%async_computation.3 | async-start | bytes 3145728 | tf_op jit(solution)/shard_map/all_to_all | solution.py:40
  301.2 93.0 %reduce-scatter.6.cloned.1.call-start = ((), (), s32[]{:S(2)}) async-start(), calls=%async_computation.6 | async-start | bytes 327680 | tf_op jit(solution)/shard_map/reduce_scatter | solution.py:162
  369.2 24.9 %copy-start.2 = (bf16[256,128]{0,1:T(8,128)(2,1)S(1)}, bf16[256,128]{0,1:T(8,128)(2,1)}, u32[]{:S(2)}) copy-start(bf16[256,128]{0,1:T(8,128)(2,1)} %reduce-scatter.4.cloned.1.call-done) | copy-start | bytes 196612
Sparse Core Ops, SparseCore 0:
  19.1 40.6 reduce-scatter.3
  194.8 91.5 all-reduce.2
  372.6 21.5 reduce-scatter.5
